TPU v7x, 128 devices: a whole 4x4x4 slice. The times are simulated.
128 devices in a mesh: blk: 8 (over z_lo, x), head: 16 (over y, z_hi, core).
Axes of the slice: x: 4, y: 4, z: 4 (z_hi: 2, z_lo: 2; z = z_hi * 2 + z_lo), core: 2. Of those that a mesh axis runs over, the one named last changes fastest.
Arguments:
- qkv: bfloat16 [32768, 6144], P(('blk', 'head')), may hold values from -12 to 12
Outputs:
- attended: bfloat16 [32768, 2048], P(('blk', 'head'))
All inputs are finite; a program needn't handle non-finite values.
Results may differ from a plain program's by a relative error of at most 0.0059.
Values may be sent and summed in bfloat16 or wider, within the bound.
A program may use at most 128 MiB of HBM per device.

v0:
```python
import jax
import jax.numpy as jnp
from jax import lax
from jax.sharding import PartitionSpec as P

HEAD_DIM = 64
BLOCK = 2048
BLK_DEV = 2


def attend(query, pair):
    keys = pair[:, 0]
    values = pair[:, 1]
    tile = min(512, BLOCK)
    scale = HEAD_DIM ** (-0.5)

    def one_tile(query_tile):
        scores = (
            jnp.einsum("qhd,khd->hqk", query_tile, keys, preferred_element_type=jnp.float32) * scale
        )
        row_max = jnp.max(scores, axis=-1)
        probs = jnp.exp(scores - row_max[..., None]).astype(jnp.bfloat16)
        total = jnp.sum(probs.astype(jnp.float32), axis=-1)
        weighted = jnp.einsum("hqk,khd->hqd", probs, values, preferred_element_type=jnp.float32)
        return (row_max, total, weighted)

    tiles = query.reshape(BLOCK // tile, tile, query.shape[1], query.shape[2])
    return lax.map(one_tile, tiles)


def combine(partials):
    overall = partials[0][0]
    for entry in partials[1:]:
        overall = jnp.maximum(overall, entry[0])
    numer = jnp.zeros_like(partials[0][2])
    denom = jnp.zeros_like(partials[0][1])
    for row_max, total, weighted in partials:
        factor = jnp.exp(row_max - overall)
        numer = numer + factor[..., None] * weighted
        denom = denom + factor * total
    result = numer / denom[..., None]
    return result.transpose(0, 2, 1, 3).reshape(BLOCK, result.shape[1] * result.shape[3])


def on_device(qkv):
    rows = qkv.shape[0]
    heads_cols = qkv.shape[1] // 3
    shaped = qkv.reshape(rows, 3, heads_cols)
    grouped = lax.all_to_all(shaped, "head", split_axis=2, concat_axis=0, tiled=True)
    local_cols = grouped.shape[2]
    heads_here = local_cols // HEAD_DIM
    grid = grouped.reshape(BLK_DEV, BLOCK, 3, heads_here, HEAD_DIM)
    queries = grid[:, :, 0]
    pairs = grid[:, :, 1:3]
    device_bits = lax.axis_size("blk").bit_length() - 1
    partials = [[] for j in range(BLK_DEV)]

    def own_blocks():
        for j in range(BLK_DEV):
            partials[j].append(attend(queries[j], pairs[j]))
            partials[j].append(attend(queries[j], pairs[j ^ 1 << 0]))

    gathered = lax.all_gather(pairs, "blk", axis=0, tiled=True)
    mine = lax.axis_index("blk")
    for bit in range(device_bits):
        for j in range(BLK_DEV):
            where = jnp.bitwise_xor(mine, 1 << bit) * BLK_DEV + j
            chosen = lax.dynamic_index_in_dim(gathered, where, 0, keepdims=False)
            partials[j].append(attend(queries[j], chosen))
    own_blocks()
    outputs = jnp.concatenate([combine(partials[j]) for j in range(BLK_DEV)], axis=0).astype(
        jnp.bfloat16
    )
    return lax.all_to_all(outputs, "head", split_axis=0, concat_axis=1, tiled=True)


def solution(mesh):
    in_specs = (P(("blk", "head"), None),)
    out_specs = P(("blk", "head"), None)
    return jax.shard_map(
        on_device, mesh=mesh, in_specs=in_specs, out_specs=out_specs, check_vma=False
    )
```

profile of v0, /device:TPU:1, one launch (start us, length us, event | category | flops | bytes accessed | tf_op | source)
XLA Modules:
  0.0 471.0 jit_solution(7720879860149030022)
XLA Ops:
  6.5 3.2 copy.39
  9.7 17.2 %copy.40 = bf16[256,3,2048]{0,1,2:T(4,128)(2,1)} copy(bf16[256,3,2048]{0,2,1:T(8,128)(2,1)S(1)} %bitcast.366) | data formatting | bytes 6291456 | tf_op jit(solution)/shard_map/reshape | solution.py:48
  26.9 9.3 %all-to-all-start = ((bf16[256,3,2048]{0,1,2:T(4,128)(2,1)}), bf16[256,3,2048]{0,1,2:T(4,128)(2,1)}, u32[]{:S(2)}, u32[]{:S(2)}) async-start(bf16[256,3,2048]{0,1,2:T(4,128)(2,1)} %copy.40), calls=%async_computation | async-start | bytes 8388608 | tf_op jit(solution)/shard_map/all_to_all | solution.py:49
  36.2 52.6 %all-to-all-done = bf16[256,3,2048]{0,1,2:T(4,128)(2,1)} async-done(((bf16[256,3,2048]{0,1,2:T(4,128)(2,1)}), bf16[256,3,2048]{0,1,2:T(4,128)(2,1)}, u32[]{:S(2)}, u32[]{:S(2)}) %all-to-all-start) | async-done | bytes 3145760 | tf_op jit(solution)/shard_map/all_to_all | solution.py:49
  91.5 3.5 copy.42
  95.0 3.9 reshape.47
  100.8 5.2 %slice_reduce_fusion.1 = (bf16[2048,2,64]{0,2,1:T(8,128)(2,1)}, bf16[2048,2,64]{0,2,1:T(8,128)(2,1)}) fusion(bf16[2,2048,3,2,64]{1,0,4,3,2:T(2,128)(2,1)S(1)} %reshape.47), kind=kLoop, calls=%fused_computation.121 | loop fusion | bytes 2097152 | tf_op jit(solution)/shard_map/slice | solution.py:69
  106.0 4.2 fusion.62
  114.7 2.9 copy_bitcast_fusion
  118.9 21.6 %while.143 = (s32[]{:T(128)}, f32[4,2,512]{2,1,0:T(2,128)S(1)}, f32[4,2,512]{2,1,0:T(2,128)S(1)}, f32[4,2,512,64]{2,3,1,0:T(8,128)}, bf16[4,512,2,64]{1,3,2,0:T(...) while((s32[]{:T(128)}, f32[4,2,512]{2,1,0:T(2,128)S(1)}, ...), condition=%wide.region_15.16_spmd, body=%wide.region_12.15_spmd.sunk | while | flops 557840384 | bytes 26640988 | solution.py:28
  141.7 21.9 %while.144 = (s32[]{:T(128)}, f32[4,2,512]{2,1,0:T(2,128)S(1)}, f32[4,2,512]{2,1,0:T(2,128)S(1)}, f32[4,2,512,64]{2,3,1,0:T(8,128)}, bf16[4,512,2,64]{1,3,2,0:T(...) while((s32[]{:T(128)}, f32[4,2,512]{2,1,0:T(2,128)S(1)}, ...), condition=%wide.region_19.20_spmd, body=%wide.region_16.19_spmd.sunk | while | flops 557840384 | bytes 26640988 | solution.py:28
  164.7 21.6 %while.148 = (s32[]{:T(128)}, f32[4,2,512]{2,1,0:T(2,128)S(1)}, f32[4,2,512]{2,1,0:T(2,128)S(1)}, f32[4,2,512,64]{2,3,1,0:T(8,128)}, bf16[4,512,2,64]{1,3,2,0:T(...) while((s32[]{:T(128)}, f32[4,2,512]{2,1,0:T(2,128)S(1)}, ...), condition=%wide.region_35.36_spmd, body=%wide.region_32.35_spmd.sunk | while | flops 557840384 | bytes 26640988 | solution.py:28
  186.9 19.9 %while.149 = (s32[]{:T(128)}, f32[4,2,512]{2,1,0:T(2,128)S(1)}, f32[4,2,512]{2,1,0:T(2,128)S(1)}, f32[4,2,512,64]{2,3,1,0:T(8,128)S(1)}, bf16[4,512,2,64]{1,3,2,...) while((s32[]{:T(128)}, f32[4,2,512]{2,1,0:T(2,128)S(1)}, ...), condition=%wide.region_39.40_spmd, body=%wide.region_36.39_spmd.sunk | while | flops 557840384 | bytes 26640480 | solution.py:28
  206.8 83.2 %all-gather.2.cloned.1.call-done = bf16[16,2048,2,2,64]{1,4,3,2,0:T(8,128)(2,1)} async-done(((bf16[2,2048,2,2,64]{1,4,3,2,0:T(8,128)(2,1)}), bf16[16,2048,2,2,64]{1,4,3,2,0:T(8,128)(2,1)}) %all-gather.2.cloned.1.call-update) | async-done | bytes 16777232 | tf_op jit(solution)/shard_map/all_gather | solution.py:63
  290.1 5.3 %dynamic-slice_bitcast_fusion.5 = (bf16[2048,2,2,64]{0,3,2,1:T(8,128)(2,1)S(1)}, bf16[2048,2,2,64]{0,3,2,1:T(8,128)(2,1)}, bf16[2048,2,2,64]{0,3,2,1:T(8,128)(2,...) fusion(bf16[16,2048,2,2,64]{1,4,3,2,0:T(8,128)(2,1)} %all-gather.2., ...), kind=kLoop, calls=%fused_computation.132 | loop fusion | bytes 12582936 | tf_op jit(solution)/shard_map/jit(dynamic_index_in_dim)/squeeze | solution.py:68
  296.9 22.0 %while.140 = (s32[]{:T(128)}, f32[4,2,512]{2,1,0:T(2,128)S(1)}, f32[4,2,512]{2,1,0:T(2,128)S(1)}, f32[4,2,512,64]{2,3,1,0:T(8,128)}, bf16[4,512,2,64]{1,3,2,0:T(...) while((s32[]{:T(128)}, f32[4,2,512]{2,1,0:T(2,128)S(1)}, ...), condition=%wide.region_3.4_spmd, body=%wide.region_0.3_spmd.sunk | while | flops 557840384 | bytes 26640988 | solution.py:28
  319.1 19.9 %while.141 = (s32[]{:T(128)}, f32[4,2,512]{2,1,0:T(2,128)S(1)}, f32[4,2,512]{2,1,0:T(2,128)S(1)}, f32[4,2,512,64]{2,3,1,0:T(8,128)S(1)}, bf16[4,512,2,64]{1,3,2,...) while((s32[]{:T(128)}, f32[4,2,512]{2,1,0:T(2,128)S(1)}, ...), condition=%wide.region_7.8_spmd, body=%wide.region_4.7_spmd.sunk | while | flops 557840384 | bytes 26640480 | solution.py:28
  342.8 21.6 %while.142 = (s32[]{:T(128)}, f32[4,2,512]{2,1,0:T(2,128)S(1)}, f32[4,2,512]{2,1,0:T(2,128)S(1)}, f32[4,2,512,64]{2,3,1,0:T(8,128)}, bf16[4,512,2,64]{1,3,2,0:T(...) while((s32[]{:T(128)}, f32[4,2,512]{2,1,0:T(2,128)S(1)}, ...), condition=%wide.region_11.12_spmd, body=%wide.region_8.11_spmd.sunk | while | flops 557840384 | bytes 26640988 | solution.py:28
  364.4 3.2 fusion.60
  368.3 20.1 %while.145 = (s32[]{:T(128)}, f32[4,2,512]{2,1,0:T(2,128)S(1)}, f32[4,2,512]{2,1,0:T(2,128)S(1)}, f32[4,2,512,64]{2,3,1,0:T(8,128)S(1)}, bf16[4,512,2,64]{1,3,2,...) while((s32[]{:T(128)}, f32[4,2,512]{2,1,0:T(2,128)S(1)}, ...), condition=%wide.region_23.24_spmd, body=%wide.region_20.23_spmd.sunk | while | flops 557840384 | bytes 26640480 | solution.py:28
  392.2 21.6 %while.146 = (s32[]{:T(128)}, f32[4,2,512]{2,1,0:T(2,128)S(1)}, f32[4,2,512]{2,1,0:T(2,128)S(1)}, f32[4,2,512,64]{2,3,1,0:T(8,128)}, bf16[4,512,2,64]{1,3,2,0:T(...) while((s32[]{:T(128)}, f32[4,2,512]{2,1,0:T(2,128)S(1)}, ...), condition=%wide.region_27.28_spmd, body=%wide.region_24.27_spmd.sunk | while | flops 557840384 | bytes 26640988 | solution.py:28
  414.0 19.9 %while.147 = (s32[]{:T(128)}, f32[4,2,512]{2,1,0:T(2,128)S(1)}, f32[4,2,512]{2,1,0:T(2,128)S(1)}, f32[4,2,512,64]{2,3,1,0:T(8,128)S(1)}, bf16[4,512,2,64]{1,3,2,...) while((s32[]{:T(128)}, f32[4,2,512]{2,1,0:T(2,128)S(1)}, ...), condition=%wide.region_31.32_spmd, body=%wide.region_28.31_spmd.sunk | while | flops 557840384 | bytes 26640480 | solution.py:28
  434.0 2.9 fusion.61
  438.2 23.8 %all_to_all.31 = bf16[16,256,128]{2,1,0:T(8,128)(2,1)S(1)} all-to-all(bf16[16,256,128]{2,1,0:T(8,128)(2,1)S(1)} %bitcast.367), channel_id=1, replica_groups=mesh['blk'=8,'head'=16] {'head'}, dimensions={0} | all-to-all | bytes 2097152 | tf_op jit(solution)/shard_map/all_to_all | solution.py:74
  (252 shorter events, 234.8 us)
Async XLA Ops:
  26.9 62.0 %all-to-all-start = ((bf16[256,3,2048]{0,1,2:T(4,128)(2,1)}), bf16[256,3,2048]{0,1,2:T(4,128)(2,1)}, u32[]{:S(2)}, u32[]{:S(2)}) async-start(bf16[256,3,2048]{0,1,2:T(4,128)(2,1)} %copy.40), calls=%async_computation | async-start | bytes 8388608 | tf_op jit(solution)/shard_map/all_to_all | solution.py:49
  36.2 253.9 %all-gather.2.cloned.1.call-start = ((), (), s32[]{:S(2)}) async-start(), calls=%async_computation.2 | async-start | bytes 18874368 | tf_op jit(solution)/shard_map/all_gather | solution.py:63
  110.2 4.5 copy-start
  140.5 1.2 copy-start.4
  140.5 1.2 copy-start.6
  163.6 1.1 copy-start.8
  163.6 1.1 copy-start.10
  186.3 0.6 copy-start.12
  186.3 0.6 copy-start.14
  206.8 88.6 %copy-start.1 = (f32[4,2,512,64]{2,3,1,0:T(8,128)}, f32[4,2,512,64]{2,3,1,0:T(8,128)S(1)}, u32[]{:S(2)}) copy-start(f32[4,2,512,64]{2,3,1,0:T(8,128)S(1)} %get-tuple-element.419) | copy-start | bytes 3145732
  206.8 88.9 %copy-start.16 = (f32[4,2,512]{2,1,0:T(2,128)}, f32[4,2,512]{2,1,0:T(2,128)S(1)}, u32[]{:S(2)}) copy-start(f32[4,2,512]{2,1,0:T(2,128)S(1)} %get-tuple-element.414) | copy-start | bytes 49156
  206.8 88.9 %copy-start.18 = (f32[4,2,512]{2,1,0:T(2,128)}, f32[4,2,512]{2,1,0:T(2,128)S(1)}, u32[]{:S(2)}) copy-start(f32[4,2,512]{2,1,0:T(2,128)S(1)} %get-tuple-element.424) | copy-start | bytes 49156
  339.0 1.0 copy-start.2
  342.7 21.6 %copy-start.5 = (f32[4,2,512]{2,1,0:T(2,128)S(1)}, f32[4,2,512]{2,1,0:T(2,128)}, u32[]{:S(2)}) copy-start(f32[4,2,512]{2,1,0:T(2,128)} %copy-done.4) | copy-start | bytes 49156
  342.7 21.6 %copy-start.7 = (f32[4,2,512]{2,1,0:T(2,128)S(1)}, f32[4,2,512]{2,1,0:T(2,128)}, u32[]{:S(2)}) copy-start(f32[4,2,512]{2,1,0:T(2,128)} %copy-done.6) | copy-start | bytes 49156
  342.8 21.6 %copy-start.9 = (f32[4,2,512]{2,1,0:T(2,128)S(1)}, f32[4,2,512]{2,1,0:T(2,128)}, u32[]{:S(2)}) copy-start(f32[4,2,512]{2,1,0:T(2,128)} %copy-done.8) | copy-start | bytes 49156
  342.8 21.6 %copy-start.11 = (f32[4,2,512]{2,1,0:T(2,128)S(1)}, f32[4,2,512]{2,1,0:T(2,128)}, u32[]{:S(2)}) copy-start(f32[4,2,512]{2,1,0:T(2,128)} %copy-done.10) | copy-start | bytes 49156
  388.4 1.0 copy-start.3
  414.0 20.0 %copy-start.13 = (f32[4,2,512]{2,1,0:T(2,128)S(1)}, f32[4,2,512]{2,1,0:T(2,128)}, u32[]{:S(2)}) copy-start(f32[4,2,512]{2,1,0:T(2,128)} %copy-done.12) | copy-start | bytes 49156
  414.0 20.0 %copy-start.15 = (f32[4,2,512]{2,1,0:T(2,128)S(1)}, f32[4,2,512]{2,1,0:T(2,128)}, u32[]{:S(2)}) copy-start(f32[4,2,512]{2,1,0:T(2,128)} %copy-done.14) | copy-start | bytes 49156
  414.0 20.0 %copy-start.17 = (f32[4,2,512]{2,1,0:T(2,128)S(1)}, f32[4,2,512]{2,1,0:T(2,128)}, u32[]{:S(2)}) copy-start(f32[4,2,512]{2,1,0:T(2,128)} %copy-done.16) | copy-start | bytes 49156
  414.0 20.0 %copy-start.19 = (f32[4,2,512]{2,1,0:T(2,128)S(1)}, f32[4,2,512]{2,1,0:T(2,128)}, u32[]{:S(2)}) copy-start(f32[4,2,512]{2,1,0:T(2,128)} %copy-done.18) | copy-start | bytes 49156
Sparse Core Ops, SparseCore 0:
  112.6 177.4 all-gather.1
where the time goes:
time: 477 us; the launch traced here: 471 us
  matrix products  142 us (30%)
  waiting for transfers between devices  136 us (29%)
  local copies, waits for them, and re-layouts  72 us (15%)
  other arithmetic  71.9 us (15%)
  blocking collectives  23.8 us (5%)
  between operations  14.1 us (3%)
  starting transfers between devices  9.34 us (2%)
    dot_general x40, matrix products, one_tile(): jnp.einsum('hqk,khd->hqd', probs, values, preferred_element_type=jnp.floa...  87 us
    all_gather x1, waiting for transfers between devices, on_device(): gathered = lax.all_gather(pairs, 'blk', axis=0, tiled=True)  83.2 us
    reduce_sum x40, other arithmetic, one_tile(): total = jnp.sum(probs.astype(jnp.float32), axis=-1)  65.6 us
    dot_general x40, matrix products, one_tile(): jnp.einsum('qhd,khd->hqk', query_tile, keys, preferred_element_type=jnp.f...  55.4 us
    all_to_all x1, waiting for transfers between devices, on_device(): lax.all_to_all(shaped, 'head', split_axis=2, concat_axis=0, tiled=True)  52.6 us
    all_to_all x1, blocking collectives, on_device(): lax.all_to_all(outputs, 'head', split_axis=0, concat_axis=1, tiled=True)  23.8 us
    reshape x1, local copies, waits for them, and re-layouts, on_device(): shaped = qkv.reshape(rows, 3, heads_cols)  17.2 us
  transfers between devices with their start and end apart: 2, of which 2 were waited for; matrix products, arithmetic and copies ran while one was open for 20% of the time, Pallas kernels for 0%

commit v1 on v0

--- a/solution.py
+++ b/solution.py
@@ -60,7 +60,9 @@
             partials[j].append(attend(queries[j], pairs[j]))
             partials[j].append(attend(queries[j], pairs[j ^ 1 << 0]))
 
-    gathered = lax.all_gather(pairs, "blk", axis=0, tiled=True)
+    gathered = jnp.concatenate(
+        lax.all_to_all(jnp.stack([pairs] * lax.axis_size("blk")), "blk", 0, 0), axis=0
+    )
     mine = lax.axis_index("blk")
     for bit in range(device_bits):
         for j in range(BLK_DEV):

time: 477 us -> 554 us (1.16)
  the two profiles are of different devices: /device:TPU:1 before, /device:TPU:6 now
where the time goes in v1:
time: 554 us; the launch traced here: 549 us
  waiting for transfers between devices  210 us (38%)
  matrix products  141 us (25%)
  local copies, waits for them, and re-layouts  78.8 us (14%)
  other arithmetic  72 us (13%)
  blocking collectives  30.2 us (5%)
  starting transfers between devices  15.1 us (3%)
    all_to_all x1, waiting for transfers between devices, on_device(): lax.all_to_all(jnp.stack([pairs] * lax.axis_size('blk')), 'blk', 0, 0)  158 us
    dot_general x40, matrix products, one_tile(): jnp.einsum('hqk,khd->hqd', probs, values, preferred_element_type=jnp.floa...  85.2 us
    reduce_sum x40, other arithmetic, one_tile(): total = jnp.sum(probs.astype(jnp.float32), axis=-1)  65.6 us
    dot_general x40, matrix products, one_tile(): jnp.einsum('qhd,khd->hqk', query_tile, keys, preferred_element_type=jnp.f...  55.4 us
    all_to_all x1, waiting for transfers between devices, on_device(): lax.all_to_all(shaped, 'head', split_axis=2, concat_axis=0, tiled=True)  52.3 us
    all_to_all x1, blocking collectives, on_device(): lax.all_to_all(outputs, 'head', split_axis=0, concat_axis=1, tiled=True)  30.2 us
    reshape x1, local copies, waits for them, and re-layouts, on_device(): shaped = qkv.reshape(rows, 3, heads_cols)  17.1 us
    unnamed x50, local copies, waits for them, and re-layouts  12.1 us
  transfers between devices with their start and end apart: 2, of which 2 were waited for; matrix products, arithmetic and copies ran while one was open for 17% of the time, Pallas kernels for 0%

profile of v1, /device:TPU:6, one launch (start us, length us, event | category | flops | bytes accessed | tf_op | source)
XLA Modules:
  0.0 549.3 jit_solution(2398714621856427508)
XLA Ops:
  3.2 17.1 %copy.42 = bf16[256,3,2048]{0,1,2:T(4,128)(2,1)} copy(bf16[256,3,2048]{0,2,1:T(8,128)(2,1)S(1)} %bitcast.367) | data formatting | bytes 6291456 | tf_op jit(solution)/shard_map/reshape | solution.py:48
  20.3 8.5 %all-to-all-start = ((bf16[256,3,2048]{0,1,2:T(4,128)(2,1)}), bf16[256,3,2048]{0,1,2:T(4,128)(2,1)}, u32[]{:S(2)}, u32[]{:S(2)}) async-start(bf16[256,3,2048]{0,1,2:T(4,128)(2,1)} %copy.42), calls=%async_computation | async-start | bytes 8388608 | tf_op jit(solution)/shard_map/all_to_all | solution.py:49
  28.8 52.3 %all-to-all-done = bf16[256,3,2048]{0,1,2:T(4,128)(2,1)} async-done(((bf16[256,3,2048]{0,1,2:T(4,128)(2,1)}), bf16[256,3,2048]{0,1,2:T(4,128)(2,1)}, u32[]{:S(2)}, u32[]{:S(2)}) %all-to-all-start) | async-done | bytes 3145760 | tf_op jit(solution)/shard_map/all_to_all | solution.py:49
  83.8 3.5 copy.44
  87.3 3.8 reshape.52
  92.9 5.2 slice_reduce_fusion.1
  98.1 4.2 fusion.62
  103.2 6.0 %stack.2 = bf16[8,2,2048,2,2,64]{2,5,4,3,1,0:T(8,128)(2,1)} broadcast(bf16[2,2048,2,2,64]{1,4,3,2,0:T(8,128)(2,1)S(1)} %copy.45), dimensions={1,2,3,4,5} | broadcast | bytes 18874368 | tf_op jit(solution)/shard_map/stack | solution.py:64
  109.2 6.6 %all-to-all-start.1 = ((bf16[8,2,2048,2,2,64]{2,5,4,3,1,0:T(8,128)(2,1)}), bf16[8,2,2048,2,2,64]{2,5,4,3,1,0:T(8,128)(2,1)}, u32[]{:S(2)}, u32[]{:S(2)}) async-start(bf16[8,2,2048,2,2,64]{2,5,4,3,1,0:T(8,128)(2,1)} %stack.2), calls=%async_computation.1 | async-start | bytes 33554432 | tf_op jit(solution)/shard_map/all_to_all | solution.py:64
  115.9 3.8 copy_bitcast_fusion
  120.0 19.9 %while.143 = (s32[]{:T(128)}, f32[4,2,512]{2,1,0:T(2,128)S(1)}, f32[4,2,512]{2,1,0:T(2,128)S(1)}, f32[4,2,512,64]{2,3,1,0:T(8,128)S(1)}, bf16[4,512,2,64]{1,3,2,...) while((s32[]{:T(128)}, f32[4,2,512]{2,1,0:T(2,128)S(1)}, ...), condition=%wide.region_15.16_spmd, body=%wide.region_12.15_spmd.sunk | while | flops 557840384 | bytes 26640480 | solution.py:28
  143.3 21.6 %while.144 = (s32[]{:T(128)}, f32[4,2,512]{2,1,0:T(2,128)S(1)}, f32[4,2,512]{2,1,0:T(2,128)S(1)}, f32[4,2,512,64]{2,3,1,0:T(8,128)}, bf16[4,512,2,64]{1,3,2,0:T(...) while((s32[]{:T(128)}, f32[4,2,512]{2,1,0:T(2,128)S(1)}, ...), condition=%wide.region_19.20_spmd, body=%wide.region_16.19_spmd.sunk | while | flops 557840384 | bytes 26640988 | solution.py:28
  167.7 21.6 %while.148 = (s32[]{:T(128)}, f32[4,2,512]{2,1,0:T(2,128)S(1)}, f32[4,2,512]{2,1,0:T(2,128)S(1)}, f32[4,2,512,64]{2,3,1,0:T(8,128)}, bf16[4,512,2,64]{1,3,2,0:T(...) while((s32[]{:T(128)}, f32[4,2,512]{2,1,0:T(2,128)S(1)}, ...), condition=%wide.region_35.36_spmd, body=%wide.region_32.35_spmd.sunk | while | flops 557840384 | bytes 26640988 | solution.py:28
  190.0 20.1 %while.149 = (s32[]{:T(128)}, f32[4,2,512]{2,1,0:T(2,128)S(1)}, f32[4,2,512]{2,1,0:T(2,128)S(1)}, f32[4,2,512,64]{2,3,1,0:T(8,128)S(1)}, bf16[4,512,2,64]{1,3,2,...) while((s32[]{:T(128)}, f32[4,2,512]{2,1,0:T(2,128)S(1)}, ...), condition=%wide.region_39.40_spmd, body=%wide.region_36.39_spmd.sunk | while | flops 557840384 | bytes 26640480 | solution.py:28
  210.1 157.9 %all-to-all-done.1 = bf16[8,2,2048,2,2,64]{2,5,4,3,1,0:T(8,128)(2,1)} async-done(((bf16[8,2,2048,2,2,64]{2,5,4,3,1,0:T(8,128)(2,1)}), bf16[8,2,2048,2,2,64]{2,5,4,3,1,0:T(8,128)(2,1)}, u32[]{:S(2)}, u32[]{:S(2)}) %all-to-all-start.1) | async-done | bytes 16777248 | tf_op jit(solution)/shard_map/all_to_all | solution.py:64
  368.0 5.2 dynamic-slice_bitcast_fusion.5
  374.7 21.7 %while.140 = (s32[]{:T(128)}, f32[4,2,512]{2,1,0:T(2,128)S(1)}, f32[4,2,512]{2,1,0:T(2,128)S(1)}, f32[4,2,512,64]{2,3,1,0:T(8,128)}, bf16[4,512,2,64]{1,3,2,0:T(...) while((s32[]{:T(128)}, f32[4,2,512]{2,1,0:T(2,128)S(1)}, ...), condition=%wide.region_3.4_spmd, body=%wide.region_0.3_spmd.sunk | while | flops 557840384 | bytes 26640988 | solution.py:28
  396.5 19.9 %while.141 = (s32[]{:T(128)}, f32[4,2,512]{2,1,0:T(2,128)S(1)}, f32[4,2,512]{2,1,0:T(2,128)S(1)}, f32[4,2,512,64]{2,3,1,0:T(8,128)S(1)}, bf16[4,512,2,64]{1,3,2,...) while((s32[]{:T(128)}, f32[4,2,512]{2,1,0:T(2,128)S(1)}, ...), condition=%wide.region_7.8_spmd, body=%wide.region_4.7_spmd.sunk | while | flops 557840384 | bytes 26640480 | solution.py:28
  420.2 22.0 %while.142 = (s32[]{:T(128)}, f32[4,2,512]{2,1,0:T(2,128)S(1)}, f32[4,2,512]{2,1,0:T(2,128)S(1)}, f32[4,2,512,64]{2,3,1,0:T(8,128)}, bf16[4,512,2,64]{1,3,2,0:T(...) while((s32[]{:T(128)}, f32[4,2,512]{2,1,0:T(2,128)S(1)}, ...), condition=%wide.region_11.12_spmd, body=%wide.region_8.11_spmd.sunk | while | flops 557840384 | bytes 26640988 | solution.py:28
  442.3 3.3 fusion.60
  447.0 19.9 %while.145 = (s32[]{:T(128)}, f32[4,2,512]{2,1,0:T(2,128)S(1)}, f32[4,2,512]{2,1,0:T(2,128)S(1)}, f32[4,2,512,64]{2,3,1,0:T(8,128)S(1)}, bf16[4,512,2,64]{1,3,2,...) while((s32[]{:T(128)}, f32[4,2,512]{2,1,0:T(2,128)S(1)}, ...), condition=%wide.region_23.24_spmd, body=%wide.region_20.23_spmd.sunk | while | flops 557840384 | bytes 26640480 | solution.py:28
  470.7 21.6 %while.146 = (s32[]{:T(128)}, f32[4,2,512]{2,1,0:T(2,128)S(1)}, f32[4,2,512]{2,1,0:T(2,128)S(1)}, f32[4,2,512,64]{2,3,1,0:T(8,128)}, bf16[4,512,2,64]{1,3,2,0:T(...) while((s32[]{:T(128)}, f32[4,2,512]{2,1,0:T(2,128)S(1)}, ...), condition=%wide.region_27.28_spmd, body=%wide.region_24.27_spmd.sunk | while | flops 557840384 | bytes 26640988 | solution.py:28
  492.5 20.1 %while.147 = (s32[]{:T(128)}, f32[4,2,512]{2,1,0:T(2,128)S(1)}, f32[4,2,512]{2,1,0:T(2,128)S(1)}, f32[4,2,512,64]{2,3,1,0:T(8,128)S(1)}, bf16[4,512,2,64]{1,3,2,...) while((s32[]{:T(128)}, f32[4,2,512]{2,1,0:T(2,128)S(1)}, ...), condition=%wide.region_31.32_spmd, body=%wide.region_28.31_spmd.sunk | while | flops 557840384 | bytes 26640480 | solution.py:28
  517.0 30.2 %all_to_all.36 = bf16[16,256,128]{2,1,0:T(8,128)(2,1)S(1)} all-to-all(bf16[16,256,128]{2,1,0:T(8,128)(2,1)S(1)} %bitcast.368), channel_id=1, replica_groups=mesh['blk'=8,'head'=16] {'head'}, dimensions={0} | all-to-all | bytes 2097152 | tf_op jit(solution)/shard_map/all_to_all | solution.py:76
  (258 shorter events, 239.2 us)
Async XLA Ops:
  20.3 60.8 %all-to-all-start = ((bf16[256,3,2048]{0,1,2:T(4,128)(2,1)}), bf16[256,3,2048]{0,1,2:T(4,128)(2,1)}, u32[]{:S(2)}, u32[]{:S(2)}) async-start(bf16[256,3,2048]{0,1,2:T(4,128)(2,1)} %copy.42), calls=%async_computation | async-start | bytes 8388608 | tf_op jit(solution)/shard_map/all_to_all | solution.py:49
  109.2 6.6 %copy-start.6 = (bf16[2048,2,64]{0,2,1:T(8,128)(2,1)S(1)}, bf16[2048,2,64]{0,2,1:T(8,128)(2,1)}, u32[]{:S(2)}) copy-start(bf16[2048,2,64]{0,2,1:T(8,128)(2,1)} %get-tuple-element.670) | copy-start | bytes 1572868
  109.2 6.7 %copy-start = (bf16[1,2048,2,2,64]{1,0,4,3,2:T(2,128)(2,1)S(1)}, bf16[1,2048,2,2,64]{1,0,4,3,2:T(2,128)(2,1)}, u32[]{:S(2)}) copy-start(bf16[1,2048,2,2,64]{1,0,4,3,2:T(2,128)(2,1)} %get-tuple-element.870) | copy-start | bytes 3145732
  109.2 258.8 %all-to-all-start.1 = ((bf16[8,2,2048,2,2,64]{2,5,4,3,1,0:T(8,128)(2,1)}), bf16[8,2,2048,2,2,64]{2,5,4,3,1,0:T(8,128)(2,1)}, u32[]{:S(2)}, u32[]{:S(2)}) async-start(bf16[8,2,2048,2,2,64]{2,5,4,3,1,0:T(8,128)(2,1)} %stack.2), calls=%async_computation.1 | async-start | bytes 33554432 | tf_op jit(solution)/shard_map/all_to_all | solution.py:64
  139.9 1.0 copy-start.1
  140.9 2.4 copy-start.7
  140.9 2.4 copy-start.9
  164.9 0.6 copy-start.13
  189.3 0.6 copy-start.15
  189.3 0.6 copy-start.17
  210.1 163.2 %copy-start.2 = (f32[4,2,512,64]{2,3,1,0:T(8,128)}, f32[4,2,512,64]{2,3,1,0:T(8,128)S(1)}, u32[]{:S(2)}) copy-start(f32[4,2,512,64]{2,3,1,0:T(8,128)S(1)} %get-tuple-element.419) | copy-start | bytes 3145732
  210.1 163.5 %copy-start.19 = (f32[4,2,512]{2,1,0:T(2,128)}, f32[4,2,512]{2,1,0:T(2,128)S(1)}, u32[]{:S(2)}) copy-start(f32[4,2,512]{2,1,0:T(2,128)S(1)} %get-tuple-element.414) | copy-start | bytes 49156
  210.1 163.5 %copy-start.21 = (f32[4,2,512]{2,1,0:T(2,128)}, f32[4,2,512]{2,1,0:T(2,128)S(1)}, u32[]{:S(2)}) copy-start(f32[4,2,512]{2,1,0:T(2,128)S(1)} %get-tuple-element.424) | copy-start | bytes 49156
  416.4 1.0 copy-start.3
  420.2 22.1 %copy-start.8 = (f32[4,2,512]{2,1,0:T(2,128)S(1)}, f32[4,2,512]{2,1,0:T(2,128)}, u32[]{:S(2)}) copy-start(f32[4,2,512]{2,1,0:T(2,128)} %copy-done.7) | copy-start | bytes 49156
  420.2 22.1 %copy-start.10 = (f32[4,2,512]{2,1,0:T(2,128)S(1)}, f32[4,2,512]{2,1,0:T(2,128)}, u32[]{:S(2)}) copy-start(f32[4,2,512]{2,1,0:T(2,128)} %copy-done.9) | copy-start | bytes 49156
  420.2 22.1 %copy-start.12 = (f32[4,2,512]{2,1,0:T(2,128)S(1)}, f32[4,2,512]{2,1,0:T(2,128)}, u32[]{:S(2)}) copy-start(f32[4,2,512]{2,1,0:T(2,128)} %copy-done.11) | copy-start | bytes 49156
  420.2 22.1 %copy-start.14 = (f32[4,2,512]{2,1,0:T(2,128)S(1)}, f32[4,2,512]{2,1,0:T(2,128)}, u32[]{:S(2)}) copy-start(f32[4,2,512]{2,1,0:T(2,128)} %copy-done.13) | copy-start | bytes 49156
  467.0 1.0 copy-start.4
  492.5 20.1 %copy-start.16 = (f32[4,2,512]{2,1,0:T(2,128)S(1)}, f32[4,2,512]{2,1,0:T(2,128)}, u32[]{:S(2)}) copy-start(f32[4,2,512]{2,1,0:T(2,128)} %copy-done.15) | copy-start | bytes 49156
  492.5 20.1 %copy-start.18 = (f32[4,2,512]{2,1,0:T(2,128)S(1)}, f32[4,2,512]{2,1,0:T(2,128)}, u32[]{:S(2)}) copy-start(f32[4,2,512]{2,1,0:T(2,128)} %copy-done.17) | copy-start | bytes 49156
  492.5 20.1 %copy-start.20 = (f32[4,2,512]{2,1,0:T(2,128)S(1)}, f32[4,2,512]{2,1,0:T(2,128)}, u32[]{:S(2)}) copy-start(f32[4,2,512]{2,1,0:T(2,128)} %copy-done.19) | copy-start | bytes 49156
  492.5 20.1 %copy-start.22 = (f32[4,2,512]{2,1,0:T(2,128)S(1)}, f32[4,2,512]{2,1,0:T(2,128)}, u32[]{:S(2)}) copy-start(f32[4,2,512]{2,1,0:T(2,128)} %copy-done.21) | copy-start | bytes 49156
  512.6 3.6 copy-start.5
  (1 other events, 0.6 us)
